TPU v7x, 256 devices: a whole 4x4x8 slice. The times are simulated.
256 devices in a mesh: cells: 64 (over x, z, core), rhs: 4 (over y).
Axes of the slice: x: 4, y: 4, z: 8, core: 2. Of those that a mesh axis runs over, the one named last changes fastest.
Arguments:
- right_side: bfloat16 [512, 512, 384], P('cells', 'rhs'), may hold values from -6 to 6
- leaf_inverse: bfloat16 [512, 384, 384], P('cells'), may hold values from -0.3125 to 0.3125
- leaf_couple: bfloat16 [512, 9, 384, 128], P('cells'), may hold values from -0.3125 to 0.3125
- skel_target: int32 [512, 9], P('cells'), may hold values from 0 to 2047, as said below
- skeleton_in: float32 [512, 2048, 128], P('rhs', 'cells'), may hold values from -6 to 6
- lift_ops: bfloat16 [64, 4096, 512], P('cells', None, 'rhs'), may hold values from -0.09375 to 0.09375
- node_mix: bfloat16 [64, 1024, 512], P('cells', None, 'rhs'), may hold values from -0.1875 to 0.1875
- node_couple: bfloat16 [64, 512, 512], P('cells', None, 'rhs'), may hold values from -0.125 to 0.125
Outputs:
- leaf_solution: bfloat16 [512, 512, 384], P('cells', 'rhs')
- skeleton_rhs: float32 [512, 2048, 128], P('rhs', 'cells')
- node_solution: bfloat16 [64, 512, 512], P('cells', 'rhs')
- node_skeleton: float32 [64, 512, 512], P('cells', 'rhs')
Inputs may be any that keep to these rules, and one draw needn't show every extreme that they name: `skel_target`: entry (c, k) names a skeleton block; its owner device, the entry // 32, lies at most 2 positions along cells from the cell's device c // 8, and on every device some slot reaches that distance.
All inputs are finite; a program needn't handle non-finite values.
Results may differ from a plain program's by a relative error of at most 0.03.
Values may be sent and summed in bfloat16 or wider, within the bound.
No kernel may reach another device: no remote copies, remote signals or barrier semaphores. Data moves between devices by JAX's collectives and lax.ppermute only.
A program may use at most 128 MiB of HBM per device.

v0:
```python
import jax
import jax.numpy as jnp
from jax import lax
from jax.sharding import PartitionSpec as P

HOP = 2


def passed_along(value, axis, steps):
    count = lax.axis_size(axis)
    initial, last = (max(0, -steps), min(count, count - steps))
    return lax.ppermute(value, axis, [(source, source + steps) for source in range(initial, last)])


def passed_along_2(value, axis, by):
    devices = lax.axis_size(axis)
    return lax.ppermute(value, axis, [(i, (i + by) % devices) for i in range(devices)])


def on_device(
    right_side, leaf_inverse, leaf_couple, skel_target, skeleton_in, lift_ops, node_mix, node_couple
):
    position = lax.axis_index("cells")
    total_devices = lax.axis_size("cells")
    levels = total_devices.bit_length() - 1
    columns = right_side.shape[1]
    blocks = skeleton_in.shape[1]
    block_width = skeleton_in.shape[2]
    solved = jnp.einsum(
        "ncr,nrq->ncq", right_side, leaf_inverse, preferred_element_type=jnp.float32
    ).astype(jnp.bfloat16)
    updates = jnp.einsum("ncr,nkrs->nkcs", solved, leaf_couple, preferred_element_type=jnp.float32)
    slot_count = updates.shape[0] * updates.shape[1]
    updates = updates.reshape(slot_count, columns, block_width)
    targets = skel_target.reshape(slot_count)
    owners = targets // blocks
    within = targets % blocks
    offsets = owners - position
    hop_reach = HOP
    span_rows = 2 * hop_reach + 1
    segment_ids = (offsets + hop_reach) * blocks + within
    summed = jax.ops.segment_sum(updates, segment_ids, num_segments=span_rows * blocks)
    portions = jnp.transpose(summed.reshape(span_rows, blocks, columns, block_width), (0, 2, 1, 3))
    arrived = portions[hop_reach]
    for distance in list(range(-hop_reach, 0)) + list(range(1, hop_reach + 1)):
        arrived = arrived + passed_along(
            portions[hop_reach + distance].astype(jnp.bfloat16), "cells", distance
        ).astype(jnp.float32)
    skeleton_rhs = skeleton_in - arrived
    gathered = (
        lax.all_gather(lift_ops[0], "rhs", axis=1, tiled=True),
        lax.all_gather(node_mix[0], "rhs", axis=1, tiled=True),
        lax.all_gather(node_couple[0], "rhs", axis=1, tiled=True),
    )

    def multiply(operand, which_op):
        return jnp.dot(operand, gathered[which_op], preferred_element_type=jnp.float32)

    def merge_node(left_child, right_child):
        joined = jnp.concatenate([left_child, right_child], axis=1)
        solution = multiply(joined, 1).astype(jnp.bfloat16)
        skeleton = 0.5 * (
            left_child.astype(jnp.float32) + right_child.astype(jnp.float32)
        ) - multiply(solution, 2)
        return (solution, skeleton)

    flattened = skeleton_rhs.reshape(columns, blocks * block_width).astype(jnp.bfloat16)
    current = multiply(flattened, 0).astype(jnp.bfloat16)
    level_solution = jnp.zeros_like(current)
    for section_level in range(1, levels + 1):
        distance = max(1, 2 ** (section_level - 2))
        left_child = passed_along_2(current, "cells", distance)
        if section_level == 1:
            right_child = current
        else:
            right_child = passed_along_2(current, "cells", -distance)
        level_solution, skeleton = merge_node(left_child, right_child)
        current = skeleton.astype(jnp.bfloat16)
    root_pair = passed_along_2(jnp.stack([current, level_solution]), "cells", -(total_devices // 2))
    node_solution, node_skeleton = merge_node(root_pair[0], root_pair[1])
    return (solved, skeleton_rhs, node_solution[None], node_skeleton[None])


def solution(mesh):
    return jax.shard_map(
        on_device,
        mesh=mesh,
        in_specs=(
            P("cells", "rhs", None),
            P("cells", None, None),
            P("cells", None, None, None),
            P("cells", None),
            P("rhs", "cells", None),
            P("cells", None, "rhs"),
            P("cells", None, "rhs"),
            P("cells", None, "rhs"),
        ),
        out_specs=(
            P("cells", "rhs", None),
            P("rhs", "cells", None),
            P("cells", "rhs", None),
            P("cells", "rhs", None),
        ),
        check_vma=False,
    )
```

profile of v0, /device:TPU:6, one launch (start us, length us, event | category | flops | bytes accessed | tf_op | source)
XLA Modules:
  0.0 207.8 jit_solution(803400362444438331)
XLA Ops:
  10.7 7.0 %fusion.27 = f32[8,128,9,128]{3,1,2,0:T(8,128)} fusion(bf16[8,9,384,128]{3,2,1,0:T(8,128)(2,1)} %param.10, bf16[8,128,384]{2,1,0:T(8,128)(2,1)S(1)} %convolution_convert_fusion), kind=kOutput, calls=%fused_computation.34 | convolution fusion | flops 905969664 | bytes 12582912 | tf_op jit(solution)/shard_map/ncr,nkrs->nkcs/dot_general | solution.py:32
  17.7 5.2 %broadcast_in_dim.10 = f32[160,128,128]{2,1,0:T(8,128)} broadcast(f32[]{:T(128)} %constant.30.clone.1), dimensions={} | broadcast | bytes 10485764 | tf_op jit(solution)/shard_map/broadcast_in_dim | solution.py:42
  22.9 17.1 %scatter_fusion = f32[160,128,128]{2,1,0:T(8,128)} fusion(f32[160,128,128]{2,1,0:T(8,128)} %broadcast_in_dim.10, s32[72]{0:T(128)S(1)} %fusion.76, f32[72,128,128]{2,1,0:T(8,128)} %bitcast.121), kind=kCustom, calls=%fused_computation | custom fusion | flops 1179648 | bytes 14156064 | tf_op jit(solution)/shard_map/scatter-add | solution.py:42
  40.0 5.4 %convert.6 = bf16[5,128,32,128]{3,1,2,0:T(8,128)(2,1)S(1)} convert(f32[5,128,32,128]{3,1,2,0:T(8,128)} %bitcast.119) | non-fusion elementwise | flops 2621440 | bytes 15728640 | tf_op jit(solution)/shard_map/convert.3
  47.5 8.0 %collective-permute-start = (bf16[128,32,128]{2,0,1:T(8,128)(2,1)}, bf16[128,32,128]{2,0,1:T(8,128)(2,1)S(1)}, u32[]{:S(2)}, u32[]{:S(2)}) collective-permute-start(bf16[128,32,128]{2,0,1:T(8,128)(2,1)} %get-tuple-element.14), channel_id=1, source_target_pairs={{8,0},{12,4},{16,8},{20,12},{24,16},{28,20},{32,24},{36,28},{40,32... | collective-permute-start | bytes 3145736 | tf_op jit(solution)/shard_map/ppermute | solution.py:12
  62.4 15.7 %collective-permute-done = bf16[128,32,128]{2,0,1:T(8,128)(2,1)S(1)} collective-permute-done((bf16[128,32,128]{2,0,1:T(8,128)(2,1)}, bf16[128,32,128]{2,0,1:T(8,128)(2,1)S(1)}, u32[]{:S(2)}, u32[]{:S(2)}) %collective-permute-start) | collective-permute-done | bytes 1048608 | tf_op jit(solution)/shard_map/ppermute | solution.py:12
  78.1 11.2 %collective-permute-done.1 = bf16[128,32,128]{2,0,1:T(8,128)(2,1)} collective-permute-done((bf16[128,32,128]{2,0,1:T(8,128)(2,1)}, bf16[128,32,128]{2,0,1:T(8,128)(2,1)}, u32[]{:S(2)}, u32[]{:S(2)}) %collective-permute-start.1) | collective-permute-done | bytes 1048608 | tf_op jit(solution)/shard_map/ppermute | solution.py:12
  90.3 6.6 %fusion.119 = (bf16[128,32,128]{2,0,1:T(8,128)(2,1)}, f32[128,32,128]{2,0,1:T(8,128)}) fusion(bf16[128,32,128]{2,0,1:T(8,128)(2,1)} %collective-permute-done.3, bf16[128,32,128]{2,0,1:T(8,128)(2,1)} %collective-permute-done.2, bf16[128,32,128]{2,0,1:T(8,128)(2,1)} %collective-permute-done.1, bf16[128,32,128]{2,0,1:T(8,128)(2,1)S(1)} %collective-permute-done, ...), kind=kLoop, calls=%fused_computation.91 | loop fusion | flops 5242880 | bytes 11534336 | tf_op jit(solution)/shard_map/convert_element_type | solution.py:67
  98.5 2.9 %fusion.7 = bf16[128,512]{1,0:T(8,128)(2,1)S(1)} fusion(bf16[128,4096]{0,1:T(8,128)(2,1)S(1)} %bitcast.122, bf16[1,4096,512]{2,1,0:T(8,128)(2,1)} %all-gather.6.cloned.1.call-done), kind=kOutput, calls=%fused_computation.10 | convolution fusion | flops 536936448 | bytes 5373952 | tf_op jit(solution)/shard_map/dot_general | solution.py:57
  101.5 8.1 %collective-permute-start.4 = (bf16[128,512]{1,0:T(8,128)(2,1)S(1)}, bf16[128,512]{1,0:T(8,128)(2,1)}, u32[]{:S(2)}, u32[]{:S(2)}) collective-permute-start(bf16[128,512]{1,0:T(8,128)(2,1)S(1)} %fusion.7), channel_id=1, source_target_pairs={{0,4},{4,8},{8,12},{12,16},{16,20},{20,24},{24,28},{28,32},{32,36}... | collective-permute-start | bytes 393224 | tf_op jit(solution)/shard_map/ppermute | solution.py:17
  109.5 15.8 %all-gather.2 = bf16[1,512,512]{2,1,0:T(8,128)(2,1)} all-gather(bf16[1,512,128]{2,1,0:T(8,128)(2,1)} %param.15), channel_id=4, replica_groups=mesh['cells'=64,'rhs'=4] {'rhs'}, dimensions={2}, use_global_device_ids=true | all-gather | bytes 655360 | tf_op jit(solution)/shard_map/all_gather | solution.py:53
  125.4 2.6 %subtract_convert_fusion.5 = bf16[128,512]{1,0:T(8,128)(2,1)} fusion(bf16[128,512]{1,0:T(8,128)(2,1)S(1)} %fusion.7, bf16[128,512]{1,0:T(8,128)(2,1)} %collective-permute-done.4, bf16[1,512,512]{2,1,0:T(8,128)(2,1)} %all-gather.2, bf16[1,1024,512]{2,1,0:T(8,128)(2,1)} %all-gather.8.cloned.1.call-done), kind=kOutput, calls=%fused_computation.73 | convolution fusion | flops 202309632 | bytes 1966080 | tf_op jit(solution)/shard_map/dot_general | solution.py:57
  128.0 3.9 %collective-permute-start.6 = (bf16[128,512]{1,0:T(8,128)(2,1)}, bf16[128,512]{1,0:T(8,128)(2,1)}, u32[]{:S(2)}, u32[]{:S(2)}) collective-permute-start(bf16[128,512]{1,0:T(8,128)(2,1)} %subtract_convert_fusion.5), channel_id=1, source_target_pairs={{0,252},{4,0},{8,4},{12,8},{16,12},{20,16},{24,20},{28,24},{32,28}... | collective-permute-start | bytes 393224 | tf_op jit(solution)/shard_map/ppermute | solution.py:17
  131.9 2.9 %collective-permute-done.5 = bf16[128,512]{1,0:T(8,128)(2,1)S(1)} collective-permute-done((bf16[128,512]{1,0:T(8,128)(2,1)}, bf16[128,512]{1,0:T(8,128)(2,1)S(1)}, u32[]{:S(2)}, u32[]{:S(2)}) %collective-permute-start.5) | collective-permute-done | bytes 131104 | tf_op jit(solution)/shard_map/ppermute | solution.py:17
  134.7 2.6 %subtract_convert_fusion.4 = bf16[128,512]{1,0:T(8,128)(2,1)} fusion(bf16[128,512]{1,0:T(8,128)(2,1)} %collective-permute-done.6, bf16[128,512]{1,0:T(8,128)(2,1)S(1)} %collective-permute-done.5, bf16[1,512,512]{2,1,0:T(8,128)(2,1)} %all-gather.2, bf16[1,1024,512]{2,1,0:T(8,128)(2,1)} %all-gather.8.cloned.1.call-done), kind=kOutput, calls=%fused_computation.72 | convolution fusion | flops 202309632 | bytes 1966080 | tf_op jit(solution)/shard_map/dot_general | solution.py:57
  137.3 4.1 %collective-permute-start.8 = (bf16[128,512]{1,0:T(8,128)(2,1)}, bf16[128,512]{1,0:T(8,128)(2,1)}, u32[]{:S(2)}, u32[]{:S(2)}) collective-permute-start(bf16[128,512]{1,0:T(8,128)(2,1)} %subtract_convert_fusion.4), channel_id=1, source_target_pairs={{0,248},{4,252},{8,0},{12,4},{16,8},{20,12},{24,16},{28,20},{32,24... | collective-permute-start | bytes 393224 | tf_op jit(solution)/shard_map/ppermute | solution.py:17
  141.4 4.1 %collective-permute-done.7 = bf16[128,512]{1,0:T(8,128)(2,1)S(1)} collective-permute-done((bf16[128,512]{1,0:T(8,128)(2,1)}, bf16[128,512]{1,0:T(8,128)(2,1)S(1)}, u32[]{:S(2)}, u32[]{:S(2)}) %collective-permute-start.7) | collective-permute-done | bytes 131104 | tf_op jit(solution)/shard_map/ppermute | solution.py:17
  150.7 4.2 %collective-permute-done.10 = bf16[128,512]{1,0:T(8,128)(2,1)S(1)} collective-permute-done((bf16[128,512]{1,0:T(8,128)(2,1)}, bf16[128,512]{1,0:T(8,128)(2,1)S(1)}, u32[]{:S(2)}, u32[]{:S(2)}) %collective-permute-start.10) | collective-permute-done | bytes 131104 | tf_op jit(solution)/shard_map/ppermute | solution.py:17
  154.9 5.9 %collective-permute-done.9 = bf16[128,512]{1,0:T(8,128)(2,1)} collective-permute-done((bf16[128,512]{1,0:T(8,128)(2,1)}, bf16[128,512]{1,0:T(8,128)(2,1)}, u32[]{:S(2)}, u32[]{:S(2)}) %collective-permute-start.9) | collective-permute-done | bytes 131104 | tf_op jit(solution)/shard_map/ppermute | solution.py:17
  163.0 6.8 %collective-permute-start.12 = (bf16[128,512]{1,0:T(8,128)(2,1)}, bf16[128,512]{1,0:T(8,128)(2,1)}, u32[]{:S(2)}, u32[]{:S(2)}) collective-permute-start(bf16[128,512]{1,0:T(8,128)(2,1)} %subtract_convert_fusion.2), channel_id=1, source_target_pairs={{0,224},{4,228},{8,232},{12,236},{16,240},{20,244},{24,248},{28,25... | collective-permute-start | bytes 393224 | tf_op jit(solution)/shard_map/ppermute | solution.py:17
  169.8 9.0 %collective-permute-done.11 = bf16[128,512]{1,0:T(8,128)(2,1)S(1)} collective-permute-done((bf16[128,512]{1,0:T(8,128)(2,1)}, bf16[128,512]{1,0:T(8,128)(2,1)S(1)}, u32[]{:S(2)}, u32[]{:S(2)}) %collective-permute-start.11) | collective-permute-done | bytes 131104 | tf_op jit(solution)/shard_map/ppermute | solution.py:17
  183.2 3.2 %collective-permute-done.13 = bf16[128,512]{1,0:T(8,128)(2,1)S(1)} collective-permute-done((bf16[128,512]{1,0:T(8,128)(2,1)}, bf16[128,512]{1,0:T(8,128)(2,1)S(1)}, u32[]{:S(2)}, u32[]{:S(2)}) %collective-permute-start.13) | collective-permute-done | bytes 131104 | tf_op jit(solution)/shard_map/ppermute | solution.py:17
  186.4 2.9 %collective-permute-done.14 = bf16[128,512]{1,0:T(8,128)(2,1)S(1)} collective-permute-done((bf16[128,512]{1,0:T(8,128)(2,1)}, bf16[128,512]{1,0:T(8,128)(2,1)S(1)}, u32[]{:S(2)}, u32[]{:S(2)}) %collective-permute-start.14) | collective-permute-done | bytes 131104 | tf_op jit(solution)/shard_map/ppermute | solution.py:17
  194.8 4.8 %collective-permute-done.15 = bf16[2,128,512]{2,1,0:T(8,128)(2,1)S(1)} collective-permute-done((bf16[2,128,512]{2,1,0:T(8,128)(2,1)S(1)}, bf16[2,128,512]{2,1,0:T(8,128)(2,1)S(1)}, u32[]{:S(2)}, u32[]{:S(2)}) %collective-permute-start.15) | collective-permute-done | bytes 262176 | tf_op jit(solution)/shard_map/ppermute | solution.py:17
  (50 shorter events, 33.5 us)
Async XLA Ops:
  7.2 1.7 copy-start
  7.2 91.3 %all-gather.6.cloned.1.call-start = ((), (), s32[]{:S(2)}) async-start(), calls=%async_computation | async-start | bytes 5242880 | tf_op jit(solution)/shard_map/all_gather | solution.py:51
  7.9 117.5 %all-gather.8.cloned.1.call-start = ((), (), s32[]{:S(2)}) async-start(), calls=%async_computation.1 | async-start | bytes 1310720 | tf_op jit(solution)/shard_map/all_gather | solution.py:52
  10.7 7.0 %copy-start.4 = (bf16[8,128,384]{2,1,0:T(8,128)(2,1)}, bf16[8,128,384]{2,1,0:T(8,128)(2,1)S(1)}, u32[]{:S(2)}) copy-start(bf16[8,128,384]{2,1,0:T(8,128)(2,1)S(1)} %convolution_convert_fusion) | copy-start | bytes 2359300
  47.5 30.6 %collective-permute-start = (bf16[128,32,128]{2,0,1:T(8,128)(2,1)}, bf16[128,32,128]{2,0,1:T(8,128)(2,1)S(1)}, u32[]{:S(2)}, u32[]{:S(2)}) collective-permute-start(bf16[128,32,128]{2,0,1:T(8,128)(2,1)} %get-tuple-element.14), channel_id=1, source_target_pairs={{8,0},{12,4},{16,8},{20,12},{24,16},{28,20},{32,24},{36,28},{40,32... | collective-permute-start | bytes 3145736 | tf_op jit(solution)/shard_map/ppermute | solution.py:12
  55.5 33.8 %collective-permute-start.1 = (bf16[128,32,128]{2,0,1:T(8,128)(2,1)}, bf16[128,32,128]{2,0,1:T(8,128)(2,1)}, u32[]{:S(2)}, u32[]{:S(2)}) collective-permute-start(bf16[128,32,128]{2,0,1:T(8,128)(2,1)} %get-tuple-element.17), channel_id=1, source_target_pairs={{4,0},{8,4},{12,8},{16,12},{20,16},{24,20},{28,24},{32,28},{36,32}... | collective-permute-start | bytes 3145736 | tf_op jit(solution)/shard_map/ppermute | solution.py:12
  57.5 31.9 %collective-permute-start.2 = (bf16[128,32,128]{2,0,1:T(8,128)(2,1)}, bf16[128,32,128]{2,0,1:T(8,128)(2,1)}, u32[]{:S(2)}, u32[]{:S(2)}) collective-permute-start(bf16[128,32,128]{2,0,1:T(8,128)(2,1)} %get-tuple-element.16), channel_id=1, source_target_pairs={{0,4},{4,8},{8,12},{12,16},{16,20},{20,24},{24,28},{28,32},{32,36}... | collective-permute-start | bytes 3145736 | tf_op jit(solution)/shard_map/ppermute | solution.py:12
  59.8 30.4 %collective-permute-start.3 = (bf16[128,32,128]{2,0,1:T(8,128)(2,1)}, bf16[128,32,128]{2,0,1:T(8,128)(2,1)}, u32[]{:S(2)}, u32[]{:S(2)}) collective-permute-start(bf16[128,32,128]{2,0,1:T(8,128)(2,1)} %get-tuple-element.15), channel_id=1, source_target_pairs={{0,8},{4,12},{8,16},{12,20},{16,24},{20,28},{24,32},{28,36},{32,40... | collective-permute-start | bytes 3145736 | tf_op jit(solution)/shard_map/ppermute | solution.py:12
  101.5 23.9 %collective-permute-start.4 = (bf16[128,512]{1,0:T(8,128)(2,1)S(1)}, bf16[128,512]{1,0:T(8,128)(2,1)}, u32[]{:S(2)}, u32[]{:S(2)}) collective-permute-start(bf16[128,512]{1,0:T(8,128)(2,1)S(1)} %fusion.7), channel_id=1, source_target_pairs={{0,4},{4,8},{8,12},{12,16},{16,20},{20,24},{24,28},{28,32},{32,36}... | collective-permute-start | bytes 393224 | tf_op jit(solution)/shard_map/ppermute | solution.py:17
  125.4 20.2 %copy-start.1 = (bf16[1,1024,512]{2,1,0:T(8,128)(2,1)S(1)}, bf16[1,1024,512]{2,1,0:T(8,128)(2,1)}, u32[]{:S(2)}) copy-start(bf16[1,1024,512]{2,1,0:T(8,128)(2,1)} %all-gather.8.cloned.1.call-done) | copy-start | bytes 3145732
  128.0 6.7 %collective-permute-start.5 = (bf16[128,512]{1,0:T(8,128)(2,1)}, bf16[128,512]{1,0:T(8,128)(2,1)S(1)}, u32[]{:S(2)}, u32[]{:S(2)}) collective-permute-start(bf16[128,512]{1,0:T(8,128)(2,1)} %subtract_convert_fusion.5), channel_id=1, source_target_pairs={{0,4},{4,8},{8,12},{12,16},{16,20},{20,24},{24,28},{28,32},{32,36}... | collective-permute-start | bytes 393224 | tf_op jit(solution)/shard_map/ppermute | solution.py:17
  128.0 6.7 %collective-permute-start.6 = (bf16[128,512]{1,0:T(8,128)(2,1)}, bf16[128,512]{1,0:T(8,128)(2,1)}, u32[]{:S(2)}, u32[]{:S(2)}) collective-permute-start(bf16[128,512]{1,0:T(8,128)(2,1)} %subtract_convert_fusion.5), channel_id=1, source_target_pairs={{0,252},{4,0},{8,4},{12,8},{16,12},{20,16},{24,20},{28,24},{32,28}... | collective-permute-start | bytes 393224 | tf_op jit(solution)/shard_map/ppermute | solution.py:17
  137.3 8.2 %collective-permute-start.7 = (bf16[128,512]{1,0:T(8,128)(2,1)}, bf16[128,512]{1,0:T(8,128)(2,1)S(1)}, u32[]{:S(2)}, u32[]{:S(2)}) collective-permute-start(bf16[128,512]{1,0:T(8,128)(2,1)} %subtract_convert_fusion.4), channel_id=1, source_target_pairs={{0,8},{4,12},{8,16},{12,20},{16,24},{20,28},{24,32},{28,36},{32,40... | collective-permute-start | bytes 393224 | tf_op jit(solution)/shard_map/ppermute | solution.py:17
  137.3 8.2 %collective-permute-start.8 = (bf16[128,512]{1,0:T(8,128)(2,1)}, bf16[128,512]{1,0:T(8,128)(2,1)}, u32[]{:S(2)}, u32[]{:S(2)}) collective-permute-start(bf16[128,512]{1,0:T(8,128)(2,1)} %subtract_convert_fusion.4), channel_id=1, source_target_pairs={{0,248},{4,252},{8,0},{12,4},{16,8},{20,12},{24,16},{28,20},{32,24... | collective-permute-start | bytes 393224 | tf_op jit(solution)/shard_map/ppermute | solution.py:17
  147.8 7.1 %collective-permute-start.10 = (bf16[128,512]{1,0:T(8,128)(2,1)}, bf16[128,512]{1,0:T(8,128)(2,1)S(1)}, u32[]{:S(2)}, u32[]{:S(2)}) collective-permute-start(bf16[128,512]{1,0:T(8,128)(2,1)} %subtract_convert_fusion.3), channel_id=1, source_target_pairs={{0,240},{4,244},{8,248},{12,252},{16,0},{20,4},{24,8},{28,12},{32,... | collective-permute-start | bytes 393224 | tf_op jit(solution)/shard_map/ppermute | solution.py:17
  148.9 11.9 %collective-permute-start.9 = (bf16[128,512]{1,0:T(8,128)(2,1)}, bf16[128,512]{1,0:T(8,128)(2,1)}, u32[]{:S(2)}, u32[]{:S(2)}) collective-permute-start(bf16[128,512]{1,0:T(8,128)(2,1)} %subtract_convert_fusion.3), channel_id=1, source_target_pairs={{0,16},{4,20},{8,24},{12,28},{16,32},{20,36},{24,40},{28,44},{32,4... | collective-permute-start | bytes 393224 | tf_op jit(solution)/shard_map/ppermute | solution.py:17
  163.0 15.9 %collective-permute-start.11 = (bf16[128,512]{1,0:T(8,128)(2,1)}, bf16[128,512]{1,0:T(8,128)(2,1)S(1)}, u32[]{:S(2)}, u32[]{:S(2)}) collective-permute-start(bf16[128,512]{1,0:T(8,128)(2,1)} %subtract_convert_fusion.2), channel_id=1, source_target_pairs={{0,32},{4,36},{8,40},{12,44},{16,48},{20,52},{24,56},{28,60},{32,6... | collective-permute-start | bytes 393224 | tf_op jit(solution)/shard_map/ppermute | solution.py:17
  163.0 15.9 %collective-permute-start.12 = (bf16[128,512]{1,0:T(8,128)(2,1)}, bf16[128,512]{1,0:T(8,128)(2,1)}, u32[]{:S(2)}, u32[]{:S(2)}) collective-permute-start(bf16[128,512]{1,0:T(8,128)(2,1)} %subtract_convert_fusion.2), channel_id=1, source_target_pairs={{0,224},{4,228},{8,232},{12,236},{16,240},{20,244},{24,248},{28,25... | collective-permute-start | bytes 393224 | tf_op jit(solution)/shard_map/ppermute | solution.py:17
  181.1 11.1 %copy-start.3 = (f32[128,32,128]{2,0,1:T(8,128)S(1)}, f32[128,32,128]{2,0,1:T(8,128)}, u32[]{:S(2)}) copy-start(f32[128,32,128]{2,0,1:T(8,128)} %get-tuple-element.13) | copy-start | bytes 6291460
  181.1 5.2 %collective-permute-start.13 = (bf16[128,512]{1,0:T(8,128)(2,1)}, bf16[128,512]{1,0:T(8,128)(2,1)S(1)}, u32[]{:S(2)}, u32[]{:S(2)}) collective-permute-start(bf16[128,512]{1,0:T(8,128)(2,1)} %subtract_convert_fusion.1), channel_id=1, source_target_pairs={{0,64},{4,68},{8,72},{12,76},{16,80},{20,84},{24,88},{28,92},{32,9... | collective-permute-start | bytes 393224 | tf_op jit(solution)/shard_map/ppermute | solution.py:17
  182.7 6.5 %collective-permute-start.14 = (bf16[128,512]{1,0:T(8,128)(2,1)}, bf16[128,512]{1,0:T(8,128)(2,1)S(1)}, u32[]{:S(2)}, u32[]{:S(2)}) collective-permute-start(bf16[128,512]{1,0:T(8,128)(2,1)} %subtract_convert_fusion.1), channel_id=1, source_target_pairs={{0,192},{4,196},{8,200},{12,204},{16,208},{20,212},{24,216},{28,22... | collective-permute-start | bytes 393224 | tf_op jit(solution)/shard_map/ppermute | solution.py:17
  189.6 10.4 %copy-start.2 = (bf16[1,512,512]{2,1,0:T(8,128)(2,1)S(1)}, bf16[1,512,512]{2,1,0:T(8,128)(2,1)}, u32[]{:S(2)}) copy-start(bf16[1,512,512]{2,1,0:T(8,128)(2,1)} %all-gather.2) | copy-start | bytes 1572868
  191.0 8.6 %collective-permute-start.15 = (bf16[2,128,512]{2,1,0:T(8,128)(2,1)S(1)}, bf16[2,128,512]{2,1,0:T(8,128)(2,1)S(1)}, u32[]{:S(2)}, u32[]{:S(2)}) collective-permute-start(bf16[2,128,512]{2,1,0:T(8,128)(2,1)S(1)} %pad_maximum_fusion), channel_id=1, source_target_pairs={{0,128},{4,132},{8,136},{12,140},{16,144},{20,148},{24,152},{28,15... | collective-permute-start | bytes 786440 | tf_op jit(solution)/shard_map/ppermute | solution.py:17
  200.0 1.0 copy-start.5
Sparse Core Ops, SparseCore 0:
  9.8 57.4 all-gather.5
  69.1 29.3 all-gather.7
where the time goes:
time: 208 us
  waiting for transfers between devices  65.6 us (32%)
  starting transfers between devices  44 us (21%)
  other arithmetic  29.1 us (14%)
  matrix products  26.6 us (13%)
  blocking collectives  15.8 us (8%)
  between operations  14.2 us (7%)
  local copies, waits for them, and re-layouts  12.4 us (6%)
    ppermute x12, waiting for transfers between devices, passed_along_2(): lax.ppermute(value, axis, [(i, (i + by) % devices) for i in range(devices)])  37 us
    ppermute x12, starting transfers between devices, passed_along_2(): lax.ppermute(value, axis, [(i, (i + by) % devices) for i in range(devices)])  29.2 us
    ppermute x4, waiting for transfers between devices, passed_along(): lax.ppermute(value, axis, [(source, source + steps) for source in range(i...  27.9 us
    dot_general x10, matrix products, multiply(): jnp.dot(operand, gathered[which_op], preferred_element_type=jnp.float32)  17.8 us
    scatter-add x1, other arithmetic, on_device(): jax.ops.segment_sum(updates, segment_ids, num_segments=span_rows * blocks)  17.1 us
    all_gather x1, blocking collectives, on_device(): lax.all_gather(node_couple[0], 'rhs', axis=1, tiled=True)  15.8 us
    ppermute x4, starting transfers between devices, passed_along(): lax.ppermute(value, axis, [(source, source + steps) for source in range(i...  14.8 us
    dot_general x1, matrix products, on_device(): jnp.einsum('ncr,nkrs->nkcs', solved, leaf_couple, preferred_element_type=...  6.99 us
  transfers between devices with their start and end apart: 18, of which 11 were waited for; matrix products, arithmetic and copies ran while one was open for 26% of the time, Pallas kernels for 0%

commit v1 on v0

--- a/solution.py
+++ b/solution.py
@@ -50,7 +50,9 @@
     gathered = (
         lax.all_gather(lift_ops[0], "rhs", axis=1, tiled=True),
         lax.all_gather(node_mix[0], "rhs", axis=1, tiled=True),
-        lax.all_gather(node_couple[0], "rhs", axis=1, tiled=True),
+        jnp.concatenate(
+            lax.all_to_all(jnp.stack([node_couple[0]] * lax.axis_size("rhs")), "rhs", 0, 0), axis=1
+        ),
     )
 
     def multiply(operand, which_op):

time: 208 us -> 202 us (0.971)
  blocking collectives: 15.8 us -> 0 us
  starting transfers between devices: 44 us -> 48.4 us
  local copies, waits for them, and re-layouts: 12.4 us -> 15 us
    all_gather x1 -> x0, blocking collectives: 15.8 us -> none  [on_device(): lax.all_gather(node_couple[0], 'rhs', axis=1, tiled=True)]
    ppermute x12, waiting for transfers between devices: 37 us -> 43 us  [passed_along_2(): lax.ppermute(value, axis, [(i, (i + by) % devices) for i in range(devices)])]
    ppermute x4, waiting for transfers between devices: 27.9 us -> 22.3 us  [passed_along(): lax.ppermute(value, axis, [(source, source + steps) for source in range(i...]
    all_to_all x0 -> x1, starting transfers between devices: none -> 4.44 us  [on_device(): lax.all_to_all(jnp.stack([node_couple[0]] * lax.axis_size('rhs')), 'rhs',...]
  transfers between devices with their start and end apart: 18 -> 19, of which waited for: 11 -> 13; matrix products, arithmetic and copies ran while one was open for 26% -> 28% of each run, Pallas kernels for 0% -> 0%
where the time goes in v1:
time: 202 us; the launch traced here: 200 us
  waiting for transfers between devices  66 us (33%)
  starting transfers between devices  48.4 us (24%)
  other arithmetic  29.5 us (15%)
  matrix products  27.2 us (13%)
  local copies, waits for them, and re-layouts  15 us (7%)
  between operations  14.2 us (7%)
    ppermute x12, waiting for transfers between devices, passed_along_2(): lax.ppermute(value, axis, [(i, (i + by) % devices) for i in range(devices)])  43 us
    ppermute x12, starting transfers between devices, passed_along_2(): lax.ppermute(value, axis, [(i, (i + by) % devices) for i in range(devices)])  28.9 us
    ppermute x4, waiting for transfers between devices, passed_along(): lax.ppermute(value, axis, [(source, source + steps) for source in range(i...  22.3 us
    dot_general x10, matrix products, multiply(): jnp.dot(operand, gathered[which_op], preferred_element_type=jnp.float32)  18.3 us
    scatter-add x1, other arithmetic, on_device(): jax.ops.segment_sum(updates, segment_ids, num_segments=span_rows * blocks)  17.2 us
    ppermute x4, starting transfers between devices, passed_along(): lax.ppermute(value, axis, [(source, source + steps) for source in range(i...  14.9 us
    dot_general x1, matrix products, on_device(): jnp.einsum('ncr,nkrs->nkcs', solved, leaf_couple, preferred_element_type=...  7.1 us
    convert_element_type x1, other arithmetic, on_device(): skeleton_rhs.reshape(columns, blocks * block_width).astype(jnp.bfloat16)  6.86 us
  transfers between devices with their start and end apart: 19, of which 13 were waited for; matrix products, arithmetic and copies ran while one was open for 28% of the time, Pallas kernels for 0%

profile of v1, /device:TPU:6, one launch (start us, length us, event | category | flops | bytes accessed | tf_op | source)
XLA Modules:
  0.0 200.2 jit_solution(6736441206878227390)
XLA Ops:
  10.7 7.1 %fusion.27 = f32[8,128,9,128]{3,1,2,0:T(8,128)} fusion(bf16[8,9,384,128]{3,2,1,0:T(8,128)(2,1)} %param.10, bf16[8,128,384]{2,1,0:T(8,128)(2,1)S(1)} %convolution_convert_fusion), kind=kOutput, calls=%fused_computation.34 | convolution fusion | flops 905969664 | bytes 12582912 | tf_op jit(solution)/shard_map/ncr,nkrs->nkcs/dot_general | solution.py:32
  17.8 5.3 %broadcast_in_dim.10 = f32[160,128,128]{2,1,0:T(8,128)} broadcast(f32[]{:T(128)} %constant.30.clone.1), dimensions={} | broadcast | bytes 10485764 | tf_op jit(solution)/shard_map/broadcast_in_dim | solution.py:42
  23.1 17.2 %scatter_fusion = f32[160,128,128]{2,1,0:T(8,128)} fusion(f32[160,128,128]{2,1,0:T(8,128)} %broadcast_in_dim.10, s32[72]{0:T(128)S(1)} %fusion.67, f32[72,128,128]{2,1,0:T(8,128)} %bitcast.110), kind=kCustom, calls=%fused_computation | custom fusion | flops 1179648 | bytes 14156064 | tf_op jit(solution)/shard_map/scatter-add | solution.py:42
  40.3 5.4 %convert.6 = bf16[5,128,32,128]{3,1,2,0:T(8,128)(2,1)S(1)} convert(f32[5,128,32,128]{3,1,2,0:T(8,128)} %bitcast.101) | non-fusion elementwise | flops 2621440 | bytes 15728640 | tf_op jit(solution)/shard_map/convert.3
  47.8 7.9 %collective-permute-start = (bf16[128,32,128]{2,0,1:T(8,128)(2,1)}, bf16[128,32,128]{2,0,1:T(8,128)(2,1)}, u32[]{:S(2)}, u32[]{:S(2)}) collective-permute-start(bf16[128,32,128]{2,0,1:T(8,128)(2,1)} %get-tuple-element.14), channel_id=1, source_target_pairs={{8,0},{12,4},{16,8},{20,12},{24,16},{28,20},{32,24},{36,28},{40,32... | collective-permute-start | bytes 3145736 | tf_op jit(solution)/shard_map/ppermute | solution.py:12
  60.1 2.6 %collective-permute-start.3 = (bf16[128,32,128]{2,0,1:T(8,128)(2,1)}, bf16[128,32,128]{2,0,1:T(8,128)(2,1)}, u32[]{:S(2)}, u32[]{:S(2)}) collective-permute-start(bf16[128,32,128]{2,0,1:T(8,128)(2,1)} %get-tuple-element.15), channel_id=1, source_target_pairs={{0,8},{4,12},{8,16},{12,20},{16,24},{20,28},{24,32},{28,36},{32,40... | collective-permute-start | bytes 3145736 | tf_op jit(solution)/shard_map/ppermute | solution.py:12
  63.8 4.4 %all-to-all-start = ((bf16[4,512,128]{1,2,0:T(8,128)(2,1)}), bf16[4,512,128]{1,2,0:T(8,128)(2,1)S(1)}, u32[]{:S(2)}, u32[]{:S(2)}) async-start(bf16[4,512,128]{1,2,0:T(8,128)(2,1)} %stack.12), calls=%async_computation | async-start | bytes 1048576 | tf_op jit(solution)/shard_map/all_to_all | solution.py:54
  68.2 10.3 %collective-permute-done = bf16[128,32,128]{2,0,1:T(8,128)(2,1)} collective-permute-done((bf16[128,32,128]{2,0,1:T(8,128)(2,1)}, bf16[128,32,128]{2,0,1:T(8,128)(2,1)}, u32[]{:S(2)}, u32[]{:S(2)}) %collective-permute-start) | collective-permute-done | bytes 1048608 | tf_op jit(solution)/shard_map/ppermute | solution.py:12
  78.5 11.2 %collective-permute-done.1 = bf16[128,32,128]{2,0,1:T(8,128)(2,1)} collective-permute-done((bf16[128,32,128]{2,0,1:T(8,128)(2,1)}, bf16[128,32,128]{2,0,1:T(8,128)(2,1)}, u32[]{:S(2)}, u32[]{:S(2)}) %collective-permute-start.1) | collective-permute-done | bytes 1048608 | tf_op jit(solution)/shard_map/ppermute | solution.py:12
  90.5 6.9 %fusion.100 = (bf16[128,32,128]{2,0,1:T(8,128)(2,1)}, f32[128,32,128]{2,0,1:T(8,128)}) fusion(bf16[128,32,128]{2,0,1:T(8,128)(2,1)} %collective-permute-done.3, bf16[128,32,128]{2,0,1:T(8,128)(2,1)} %collective-permute-done.2, bf16[128,32,128]{2,0,1:T(8,128)(2,1)} %collective-permute-done.1, bf16[128,32,128]{2,0,1:T(8,128)(2,1)} %collective-permute-done, ...), kind=kLoop, calls=%fused_computation.82 | loop fusion | flops 5242880 | bytes 11534336 | tf_op jit(solution)/shard_map/convert_element_type | solution.py:69
  99.6 3.3 %fusion.7 = bf16[128,512]{1,0:T(8,128)(2,1)S(1)} fusion(bf16[128,4096]{0,1:T(8,128)(2,1)} %bitcast.111, bf16[1,4096,512]{2,1,0:T(8,128)(2,1)} %all-gather.5.cloned.1.call-done), kind=kOutput, calls=%fused_computation.10 | convolution fusion | flops 536936448 | bytes 5373952 | tf_op jit(solution)/shard_map/dot_general | solution.py:59
  102.9 8.2 %collective-permute-start.4 = (bf16[128,512]{1,0:T(8,128)(2,1)S(1)}, bf16[128,512]{1,0:T(8,128)(2,1)}, u32[]{:S(2)}, u32[]{:S(2)}) collective-permute-start(bf16[128,512]{1,0:T(8,128)(2,1)S(1)} %fusion.7), channel_id=1, source_target_pairs={{0,4},{4,8},{8,12},{12,16},{16,20},{20,24},{24,28},{28,32},{32,36}... | collective-permute-start | bytes 393224 | tf_op jit(solution)/shard_map/ppermute | solution.py:17
  113.3 2.6 %subtract_convert_fusion.5 = bf16[128,512]{1,0:T(8,128)(2,1)} fusion(bf16[128,512]{1,0:T(8,128)(2,1)S(1)} %fusion.7, bf16[128,512]{1,0:T(8,128)(2,1)} %collective-permute-done.4, bf16[512,512]{0,1:T(8,128)(2,1)} %bitcast.103, bf16[1,1024,512]{2,1,0:T(8,128)(2,1)} %all-gather.7.cloned.1.call-done), kind=kOutput, calls=%fused_computation.64 | convolution fusion | flops 202309632 | bytes 1966080 | tf_op jit(solution)/shard_map/dot_general | solution.py:59
  115.9 3.9 %collective-permute-start.6 = (bf16[128,512]{1,0:T(8,128)(2,1)}, bf16[128,512]{1,0:T(8,128)(2,1)}, u32[]{:S(2)}, u32[]{:S(2)}) collective-permute-start(bf16[128,512]{1,0:T(8,128)(2,1)} %subtract_convert_fusion.5), channel_id=1, source_target_pairs={{0,252},{4,0},{8,4},{12,8},{16,12},{20,16},{24,20},{28,24},{32,28}... | collective-permute-start | bytes 393224 | tf_op jit(solution)/shard_map/ppermute | solution.py:17
  119.7 2.9 %collective-permute-done.5 = bf16[128,512]{1,0:T(8,128)(2,1)S(1)} collective-permute-done((bf16[128,512]{1,0:T(8,128)(2,1)}, bf16[128,512]{1,0:T(8,128)(2,1)S(1)}, u32[]{:S(2)}, u32[]{:S(2)}) %collective-permute-start.5) | collective-permute-done | bytes 131104 | tf_op jit(solution)/shard_map/ppermute | solution.py:17
  125.3 4.1 %collective-permute-start.8 = (bf16[128,512]{1,0:T(8,128)(2,1)}, bf16[128,512]{1,0:T(8,128)(2,1)}, u32[]{:S(2)}, u32[]{:S(2)}) collective-permute-start(bf16[128,512]{1,0:T(8,128)(2,1)} %subtract_convert_fusion.4), channel_id=1, source_target_pairs={{0,248},{4,252},{8,0},{12,4},{16,8},{20,12},{24,16},{28,20},{32,24... | collective-permute-start | bytes 393224 | tf_op jit(solution)/shard_map/ppermute | solution.py:17
  129.3 4.1 %collective-permute-done.7 = bf16[128,512]{1,0:T(8,128)(2,1)S(1)} collective-permute-done((bf16[128,512]{1,0:T(8,128)(2,1)}, bf16[128,512]{1,0:T(8,128)(2,1)S(1)}, u32[]{:S(2)}, u32[]{:S(2)}) %collective-permute-start.7) | collective-permute-done | bytes 131104 | tf_op jit(solution)/shard_map/ppermute | solution.py:17
  138.6 5.5 %collective-permute-done.10 = bf16[128,512]{1,0:T(8,128)(2,1)S(1)} collective-permute-done((bf16[128,512]{1,0:T(8,128)(2,1)}, bf16[128,512]{1,0:T(8,128)(2,1)S(1)}, u32[]{:S(2)}, u32[]{:S(2)}) %collective-permute-start.10) | collective-permute-done | bytes 131104 | tf_op jit(solution)/shard_map/ppermute | solution.py:17
  144.1 4.6 %collective-permute-done.9 = bf16[128,512]{1,0:T(8,128)(2,1)} collective-permute-done((bf16[128,512]{1,0:T(8,128)(2,1)}, bf16[128,512]{1,0:T(8,128)(2,1)}, u32[]{:S(2)}, u32[]{:S(2)}) %collective-permute-start.9) | collective-permute-done | bytes 131104 | tf_op jit(solution)/shard_map/ppermute | solution.py:17
  151.0 6.8 %collective-permute-start.12 = (bf16[128,512]{1,0:T(8,128)(2,1)}, bf16[128,512]{1,0:T(8,128)(2,1)}, u32[]{:S(2)}, u32[]{:S(2)}) collective-permute-start(bf16[128,512]{1,0:T(8,128)(2,1)} %subtract_convert_fusion.2), channel_id=1, source_target_pairs={{0,224},{4,228},{8,232},{12,236},{16,240},{20,244},{24,248},{28,25... | collective-permute-start | bytes 393224 | tf_op jit(solution)/shard_map/ppermute | solution.py:17
  157.8 7.7 %collective-permute-done.11 = bf16[128,512]{1,0:T(8,128)(2,1)S(1)} collective-permute-done((bf16[128,512]{1,0:T(8,128)(2,1)}, bf16[128,512]{1,0:T(8,128)(2,1)S(1)}, u32[]{:S(2)}, u32[]{:S(2)}) %collective-permute-start.11) | collective-permute-done | bytes 131104 | tf_op jit(solution)/shard_map/ppermute | solution.py:17
  165.5 6.6 %collective-permute-done.12 = bf16[128,512]{1,0:T(8,128)(2,1)} collective-permute-done((bf16[128,512]{1,0:T(8,128)(2,1)}, bf16[128,512]{1,0:T(8,128)(2,1)}, u32[]{:S(2)}, u32[]{:S(2)}) %collective-permute-start.12) | collective-permute-done | bytes 131104 | tf_op jit(solution)/shard_map/ppermute | solution.py:17
  176.4 3.6 %collective-permute-done.13 = bf16[128,512]{1,0:T(8,128)(2,1)S(1)} collective-permute-done((bf16[128,512]{1,0:T(8,128)(2,1)}, bf16[128,512]{1,0:T(8,128)(2,1)S(1)}, u32[]{:S(2)}, u32[]{:S(2)}) %collective-permute-start.13) | collective-permute-done | bytes 131104 | tf_op jit(solution)/shard_map/ppermute | solution.py:17
  186.5 5.5 %collective-permute-done.15 = bf16[2,128,512]{2,1,0:T(8,128)(2,1)S(1)} collective-permute-done((bf16[2,128,512]{2,1,0:T(8,128)(2,1)S(1)}, bf16[2,128,512]{2,1,0:T(8,128)(2,1)S(1)}, u32[]{:S(2)}, u32[]{:S(2)}) %collective-permute-start.15) | collective-permute-done | bytes 262176 | tf_op jit(solution)/shard_map/ppermute | solution.py:17
  (57 shorter events, 38.4 us)
Async XLA Ops:
  7.2 92.5 %all-gather.5.cloned.1.call-start = ((), (), s32[]{:S(2)}) async-start(), calls=%async_computation.1 | async-start | bytes 5242880 | tf_op jit(solution)/shard_map/all_gather | solution.py:51
  7.9 104.0 %all-gather.7.cloned.1.call-start = ((), (), s32[]{:S(2)}) async-start(), calls=%async_computation.2 | async-start | bytes 1310720 | tf_op jit(solution)/shard_map/all_gather | solution.py:52
  10.7 7.1 %copy-start.5 = (bf16[8,128,384]{2,1,0:T(8,128)(2,1)}, bf16[8,128,384]{2,1,0:T(8,128)(2,1)S(1)}, u32[]{:S(2)}) copy-start(bf16[8,128,384]{2,1,0:T(8,128)(2,1)S(1)} %convolution_convert_fusion) | copy-start | bytes 2359300
  45.7 17.1 %copy-start.7 = (bf16[1,512,128]{2,1,0:T(8,128)(2,1)S(1)}, bf16[1,512,128]{2,1,0:T(8,128)(2,1)}, u32[]{:S(2)}) copy-start(bf16[1,512,128]{2,1,0:T(8,128)(2,1)} %param.15) | copy-start | bytes 393220
  47.8 30.7 %collective-permute-start = (bf16[128,32,128]{2,0,1:T(8,128)(2,1)}, bf16[128,32,128]{2,0,1:T(8,128)(2,1)}, u32[]{:S(2)}, u32[]{:S(2)}) collective-permute-start(bf16[128,32,128]{2,0,1:T(8,128)(2,1)} %get-tuple-element.14), channel_id=1, source_target_pairs={{8,0},{12,4},{16,8},{20,12},{24,16},{28,20},{32,24},{36,28},{40,32... | collective-permute-start | bytes 3145736 | tf_op jit(solution)/shard_map/ppermute | solution.py:12
  55.7 34.0 %collective-permute-start.1 = (bf16[128,32,128]{2,0,1:T(8,128)(2,1)}, bf16[128,32,128]{2,0,1:T(8,128)(2,1)}, u32[]{:S(2)}, u32[]{:S(2)}) collective-permute-start(bf16[128,32,128]{2,0,1:T(8,128)(2,1)} %get-tuple-element.17), channel_id=1, source_target_pairs={{4,0},{8,4},{12,8},{16,12},{20,16},{24,20},{28,24},{32,28},{36,32}... | collective-permute-start | bytes 3145736 | tf_op jit(solution)/shard_map/ppermute | solution.py:12
  57.8 32.0 %collective-permute-start.2 = (bf16[128,32,128]{2,0,1:T(8,128)(2,1)}, bf16[128,32,128]{2,0,1:T(8,128)(2,1)}, u32[]{:S(2)}, u32[]{:S(2)}) collective-permute-start(bf16[128,32,128]{2,0,1:T(8,128)(2,1)} %get-tuple-element.16), channel_id=1, source_target_pairs={{0,4},{4,8},{8,12},{12,16},{16,20},{20,24},{24,28},{28,32},{32,36}... | collective-permute-start | bytes 3145736 | tf_op jit(solution)/shard_map/ppermute | solution.py:12
  60.1 30.4 %collective-permute-start.3 = (bf16[128,32,128]{2,0,1:T(8,128)(2,1)}, bf16[128,32,128]{2,0,1:T(8,128)(2,1)}, u32[]{:S(2)}, u32[]{:S(2)}) collective-permute-start(bf16[128,32,128]{2,0,1:T(8,128)(2,1)} %get-tuple-element.15), channel_id=1, source_target_pairs={{0,8},{4,12},{8,16},{12,20},{16,24},{20,28},{24,32},{28,36},{32,40... | collective-permute-start | bytes 3145736 | tf_op jit(solution)/shard_map/ppermute | solution.py:12
  63.8 47.3 %all-to-all-start = ((bf16[4,512,128]{1,2,0:T(8,128)(2,1)}), bf16[4,512,128]{1,2,0:T(8,128)(2,1)S(1)}, u32[]{:S(2)}, u32[]{:S(2)}) async-start(bf16[4,512,128]{1,2,0:T(8,128)(2,1)} %stack.12), calls=%async_computation | async-start | bytes 1048576 | tf_op jit(solution)/shard_map/all_to_all | solution.py:54
  102.9 10.4 %collective-permute-start.4 = (bf16[128,512]{1,0:T(8,128)(2,1)S(1)}, bf16[128,512]{1,0:T(8,128)(2,1)}, u32[]{:S(2)}, u32[]{:S(2)}) collective-permute-start(bf16[128,512]{1,0:T(8,128)(2,1)S(1)} %fusion.7), channel_id=1, source_target_pairs={{0,4},{4,8},{8,12},{12,16},{16,20},{20,24},{24,28},{28,32},{32,36}... | collective-permute-start | bytes 393224 | tf_op jit(solution)/shard_map/ppermute | solution.py:17
  111.9 21.5 %copy-start.1 = (bf16[1,1024,512]{2,1,0:T(8,128)(2,1)S(1)}, bf16[1,1024,512]{2,1,0:T(8,128)(2,1)}, u32[]{:S(2)}) copy-start(bf16[1,1024,512]{2,1,0:T(8,128)(2,1)} %all-gather.7.cloned.1.call-done) | copy-start | bytes 3145732
  115.9 6.7 %collective-permute-start.5 = (bf16[128,512]{1,0:T(8,128)(2,1)}, bf16[128,512]{1,0:T(8,128)(2,1)S(1)}, u32[]{:S(2)}, u32[]{:S(2)}) collective-permute-start(bf16[128,512]{1,0:T(8,128)(2,1)} %subtract_convert_fusion.5), channel_id=1, source_target_pairs={{0,4},{4,8},{8,12},{12,16},{16,20},{20,24},{24,28},{28,32},{32,36}... | collective-permute-start | bytes 393224 | tf_op jit(solution)/shard_map/ppermute | solution.py:17
  115.9 6.7 %collective-permute-start.6 = (bf16[128,512]{1,0:T(8,128)(2,1)}, bf16[128,512]{1,0:T(8,128)(2,1)}, u32[]{:S(2)}, u32[]{:S(2)}) collective-permute-start(bf16[128,512]{1,0:T(8,128)(2,1)} %subtract_convert_fusion.5), channel_id=1, source_target_pairs={{0,252},{4,0},{8,4},{12,8},{16,12},{20,16},{24,20},{28,24},{32,28}... | collective-permute-start | bytes 393224 | tf_op jit(solution)/shard_map/ppermute | solution.py:17
  125.2 8.2 %collective-permute-start.7 = (bf16[128,512]{1,0:T(8,128)(2,1)}, bf16[128,512]{1,0:T(8,128)(2,1)S(1)}, u32[]{:S(2)}, u32[]{:S(2)}) collective-permute-start(bf16[128,512]{1,0:T(8,128)(2,1)} %subtract_convert_fusion.4), channel_id=1, source_target_pairs={{0,8},{4,12},{8,16},{12,20},{16,24},{20,28},{24,32},{28,36},{32,40... | collective-permute-start | bytes 393224 | tf_op jit(solution)/shard_map/ppermute | solution.py:17
  125.3 8.2 %collective-permute-start.8 = (bf16[128,512]{1,0:T(8,128)(2,1)}, bf16[128,512]{1,0:T(8,128)(2,1)}, u32[]{:S(2)}, u32[]{:S(2)}) collective-permute-start(bf16[128,512]{1,0:T(8,128)(2,1)} %subtract_convert_fusion.4), channel_id=1, source_target_pairs={{0,248},{4,252},{8,0},{12,4},{16,8},{20,12},{24,16},{28,20},{32,24... | collective-permute-start | bytes 393224 | tf_op jit(solution)/shard_map/ppermute | solution.py:17
  135.7 8.4 %collective-permute-start.10 = (bf16[128,512]{1,0:T(8,128)(2,1)}, bf16[128,512]{1,0:T(8,128)(2,1)S(1)}, u32[]{:S(2)}, u32[]{:S(2)}) collective-permute-start(bf16[128,512]{1,0:T(8,128)(2,1)} %subtract_convert_fusion.3), channel_id=1, source_target_pairs={{0,240},{4,244},{8,248},{12,252},{16,0},{20,4},{24,8},{28,12},{32,... | collective-permute-start | bytes 393224 | tf_op jit(solution)/shard_map/ppermute | solution.py:17
  136.8 11.9 %collective-permute-start.9 = (bf16[128,512]{1,0:T(8,128)(2,1)}, bf16[128,512]{1,0:T(8,128)(2,1)}, u32[]{:S(2)}, u32[]{:S(2)}) collective-permute-start(bf16[128,512]{1,0:T(8,128)(2,1)} %subtract_convert_fusion.3), channel_id=1, source_target_pairs={{0,16},{4,20},{8,24},{12,28},{16,32},{20,36},{24,40},{28,44},{32,4... | collective-permute-start | bytes 393224 | tf_op jit(solution)/shard_map/ppermute | solution.py:17
  151.0 14.5 %collective-permute-start.11 = (bf16[128,512]{1,0:T(8,128)(2,1)}, bf16[128,512]{1,0:T(8,128)(2,1)S(1)}, u32[]{:S(2)}, u32[]{:S(2)}) collective-permute-start(bf16[128,512]{1,0:T(8,128)(2,1)} %subtract_convert_fusion.2), channel_id=1, source_target_pairs={{0,32},{4,36},{8,40},{12,44},{16,48},{20,52},{24,56},{28,60},{32,6... | collective-permute-start | bytes 393224 | tf_op jit(solution)/shard_map/ppermute | solution.py:17
  151.0 21.1 %collective-permute-start.12 = (bf16[128,512]{1,0:T(8,128)(2,1)}, bf16[128,512]{1,0:T(8,128)(2,1)}, u32[]{:S(2)}, u32[]{:S(2)}) collective-permute-start(bf16[128,512]{1,0:T(8,128)(2,1)} %subtract_convert_fusion.2), channel_id=1, source_target_pairs={{0,224},{4,228},{8,232},{12,236},{16,240},{20,244},{24,248},{28,25... | collective-permute-start | bytes 393224 | tf_op jit(solution)/shard_map/ppermute | solution.py:17
  174.4 9.6 %copy-start.4 = (f32[128,32,128]{2,0,1:T(8,128)S(1)}, f32[128,32,128]{2,0,1:T(8,128)}, u32[]{:S(2)}) copy-start(f32[128,32,128]{2,0,1:T(8,128)} %get-tuple-element.13) | copy-start | bytes 6291460
  174.4 5.6 %collective-permute-start.13 = (bf16[128,512]{1,0:T(8,128)(2,1)}, bf16[128,512]{1,0:T(8,128)(2,1)S(1)}, u32[]{:S(2)}, u32[]{:S(2)}) collective-permute-start(bf16[128,512]{1,0:T(8,128)(2,1)} %subtract_convert_fusion.1), channel_id=1, source_target_pairs={{0,64},{4,68},{8,72},{12,76},{16,80},{20,84},{24,88},{28,92},{32,9... | collective-permute-start | bytes 393224 | tf_op jit(solution)/shard_map/ppermute | solution.py:17
  174.4 6.8 %collective-permute-start.14 = (bf16[128,512]{1,0:T(8,128)(2,1)}, bf16[128,512]{1,0:T(8,128)(2,1)S(1)}, u32[]{:S(2)}, u32[]{:S(2)}) collective-permute-start(bf16[128,512]{1,0:T(8,128)(2,1)} %subtract_convert_fusion.1), channel_id=1, source_target_pairs={{0,192},{4,196},{8,200},{12,204},{16,208},{20,212},{24,216},{28,22... | collective-permute-start | bytes 393224 | tf_op jit(solution)/shard_map/ppermute | solution.py:17
  181.6 10.8 %copy-start.3 = (bf16[4,512,128]{1,2,0:T(8,128)(2,1)S(1)}, bf16[4,512,128]{1,2,0:T(8,128)(2,1)}, u32[]{:S(2)}) copy-start(bf16[4,512,128]{1,2,0:T(8,128)(2,1)} %copy-done.2) | copy-start | bytes 1572868
  183.0 9.0 %collective-permute-start.15 = (bf16[2,128,512]{2,1,0:T(8,128)(2,1)S(1)}, bf16[2,128,512]{2,1,0:T(8,128)(2,1)S(1)}, u32[]{:S(2)}, u32[]{:S(2)}) collective-permute-start(bf16[2,128,512]{2,1,0:T(8,128)(2,1)S(1)} %pad_maximum_fusion), channel_id=1, source_target_pairs={{0,128},{4,132},{8,136},{12,140},{16,144},{20,148},{24,152},{28,15... | collective-permute-start | bytes 786440 | tf_op jit(solution)/shard_map/ppermute | solution.py:17
  (3 other events, 3.5 us)
Sparse Core Ops, SparseCore 0:
  9.8 57.4 all-gather.4
  69.1 29.3 all-gather.6
